TPU v7x, 32 devices: a whole 2x2x4 slice. The times are simulated.
32 devices in a mesh: tile: 8 (over z, x), depth: 4 (over y, core).
Axes of the slice: x: 2, y: 2, z: 4, core: 2. Of those that a mesh axis runs over, the one named last changes fastest.
Arguments:
- density: float32 [64, 128, 128], P('depth', 'tile'), may hold values from 0.5 to 2
- momentum: float32 [3, 64, 128, 128], P(None, 'depth', 'tile'), may hold values from -4 to 4
- magnetic: float32 [3, 64, 128, 128], P(None, 'depth', 'tile'), may hold values from -4 to 4
- energy: float32 [64, 128, 128], P('depth', 'tile'), may hold values from 2 to 4
- shifts: int32 [24], replicated, may hold values from 0 to 55, as said below
- levels: int32 [24], replicated, may hold values from 0 to 63, as said below
Outputs:
- new_state: float32 [8, 64, 128, 128], P(None, 'depth', 'tile')
- intensity: float32 [48, 128, 128], P(None, 'tile', 'depth')
Inputs may be any that keep to these rules, and one draw needn't show every extreme that they name: shifts[k] = (1732 (levels[k] - levels[0]) + 1000) // 2000, the nearest whole column to tan(60 degrees) times the depth gap at half a column per level; the last is exactly 55. 24 distinct levels in ascending order, the first 0 and the last 63; each depth slab of 16 consecutive levels holds at most 8 of them, and some slab exactly 8.
All inputs are finite; a program needn't handle non-finite values.
Results may differ from a plain program's by a relative error of at most 0.000054.
Values sent between devices are 32-bit elements; how exact they have to be, the bound alone decides.
A program may use at most 64 MiB of HBM per device.

v0:
```python
import jax
import jax.numpy as jnp
from jax import lax
from jax.sharding import PartitionSpec as P

W = 48
GAMMA = 5.0 / 3.0
SECTION = 0.02
GRAVITY = 0.5
SIN_VIEW = 0.8660254037844386
COS_VIEW = 0.5
STRENGTH = 4.0
SPACING = 0.25


def shifted(block, axis, distance):
    devices = range(lax.axis_size(axis))
    route = [((i - distance) % len(devices), i) for i in devices]
    return lax.ppermute(block, axis, route)


def padded_2(cells, sides, width, closed):
    for axis, dim in sides:
        count = lax.axis_size(axis)
        ends = count if closed else count - 1
        head = lax.slice_in_dim(cells, 0, width, axis=dim)
        tail = lax.slice_in_dim(cells, cells.shape[dim] - width, cells.shape[dim], axis=dim)
        cells = jnp.concatenate(
            [
                lax.ppermute(tail, axis, [(i, (i + 1) % count) for i in range(ends)]),
                cells,
                lax.ppermute(head, axis, [((i + 1) % count, i) for i in range(ends)]),
            ],
            axis=dim,
        )
    return cells


def derive(padded, axis, count):

    def layer(offset):
        return lax.slice_in_dim(padded, offset, offset + count, axis=axis)

    return (
        45.0 * (layer(4) - layer(2)) - 9.0 * (layer(5) - layer(1)) + (layer(6) - layer(0))
    ) / 60.0


def flux(state, comp):
    rho = state[0]
    moment = state[1:4]
    field = state[4:7]
    energy = state[7]
    velocity = moment / rho
    field_sq = jnp.sum(field * field, axis=0)
    pressure = (GAMMA - 1.0) * (energy - 0.5 * jnp.sum(moment * velocity, axis=0) - 0.5 * field_sq)
    total = pressure + 0.5 * field_sq
    along = velocity[comp]
    normal = field[comp]
    flux_mom = (moment * along - field * normal).at[comp].add(total)
    flux_mag = along * field - normal * velocity
    flux_energy = (energy + total) * along - normal * jnp.sum(velocity * field, axis=0)
    return jnp.concatenate([moment[comp][None], flux_mom, flux_mag, flux_energy[None]], axis=0)


def tendency(along_x, along_y, along_z, state):
    depth_cells, width_cells, cross_cells = (state.shape[1], state.shape[2], state.shape[3])
    rate = -(
        derive(flux(along_x, 0), 2, width_cells)
        + derive(flux(along_y, 1), 3, cross_cells)
        + derive(flux(along_z, 2), 1, depth_cells)
    )
    rate = rate.at[3].add(GRAVITY * state[0])
    rate = rate.at[7].add(GRAVITY * state[3])
    return rate


def line_fields(new_state):
    dens = 0.5 + jax.nn.softplus(new_state[0])
    speed = (COS_VIEW * new_state[3] + SIN_VIEW * new_state[1]) / dens
    field_sq = jnp.sum(new_state[4:7] * new_state[4:7], axis=0)
    source = jax.nn.softplus(new_state[7] - 0.5 * field_sq) / dens
    return jnp.stack([dens, speed, source], axis=1)


def rows_mask(flags):
    return flags[:, None, None, None]


def shear(rows, row_shift, reach):
    cells = rows.shape[2]
    tiles_ahead = row_shift // cells
    offset = row_shift % cells

    def advance(turn, carry):
        piece, near, beyond = carry
        piece = shifted(piece, "tile", -1)
        near = jnp.where(rows_mask(tiles_ahead == turn), piece, near)
        beyond = jnp.where(rows_mask(tiles_ahead + 1 == turn), piece, beyond)
        return (piece, near, beyond)

    start_near = jnp.where(rows_mask(tiles_ahead == 0), rows, jnp.zeros_like(rows))
    carry = lax.fori_loop(1, reach + 2, advance, (rows, start_near, jnp.zeros_like(rows)))
    near = carry[1]
    beyond = carry[2]
    joined = jnp.concatenate([near, beyond], axis=2)
    target = jnp.arange(cells, dtype=jnp.int32)
    anchor = jnp.arange(2 * cells, dtype=jnp.int32)
    select = (anchor[None, None, :] == target[None, :, None] + offset[:, None, None]).astype(
        jnp.float32
    )
    return jnp.einsum("lcxa,lwx->lcwa", joined, select, precision=lax.Precision.HIGHEST)


def regroup(rows):
    return lax.all_to_all(rows, "depth", split_axis=3, concat_axis=0, tiled=True)


def emergent(columns):
    positions = columns.shape[0]
    flat = columns.reshape(positions, 3, -1)
    dens = flat[:, 0]
    speed = flat[:, 1]
    source = flat[:, 2]
    waves = (jnp.arange(W, dtype=jnp.float32) - 0.5 * (W - 1)) * SPACING
    gap = waves[:, None, None] - speed[None]
    dtau = 2.0 / positions * dens[None] * (1.0 + STRENGTH * jnp.exp(-gap * gap))
    order = jnp.arange(positions, dtype=jnp.int32)
    earlier = (order[None, :] < order[:, None]).astype(jnp.float32)
    above = jnp.einsum("kj,wjc->wkc", earlier, dtau, precision=lax.Precision.HIGHEST)
    inner = jnp.sum(source[None] * jnp.exp(-above) * (1.0 - jnp.exp(-dtau)), axis=1)
    total = inner + source[-1][None] * jnp.exp(-above[:, -1] - dtau[:, -1])
    return total.reshape((W,) + columns.shape[2:])


def per_device(density, momentum, magnetic, energy, shifts, levels):
    state = jnp.concatenate([density[None], momentum, magnetic, energy[None]], axis=0)
    count_vars, depth_cells, width_cells, cross_cells = state.shape
    depth_at = lax.axis_index("depth")
    slabs = lax.axis_size("depth")
    along_x = padded_2(state, (("tile", 2),), 3, True)
    padded = padded_2(state, (("depth", 1),), 3, False)
    rim_shape = (count_vars, 3, width_cells, cross_cells)
    head = jnp.where(depth_at == 0, jnp.broadcast_to(state[:, :1], rim_shape), padded[:, :3])
    tail = jnp.where(
        depth_at == slabs - 1,
        jnp.broadcast_to(state[:, -1:], rim_shape),
        padded[:, depth_cells + 3 :],
    )
    along_z = jnp.concatenate([head, state, tail], axis=1)
    along_y = jnp.pad(state, ((0, 0), (0, 0), (0, 0), (3, 3)), mode="wrap")
    new_state = state + SECTION * tendency(along_x, along_y, along_z, state)
    fields = line_fields(new_state)
    largest = (1732 * (depth_cells * slabs - 1) + 1000) // 2000
    reach = largest // width_cells
    lowest = depth_at * depth_cells
    local_level = lowest + jnp.arange(depth_cells, dtype=jnp.int32)
    match = local_level[:, None] == levels[None, :]
    level_shift = jnp.sum(jnp.where(match, shifts[None, :], 0), axis=1)
    columns = regroup(shear(fields, level_shift, reach))[levels]
    intensity = emergent(columns)
    return (new_state, intensity)


def solution(mesh):
    return jax.shard_map(
        per_device,
        mesh=mesh,
        in_specs=(
            P("depth", "tile", None),
            P(None, "depth", "tile", None),
            P(None, "depth", "tile", None),
            P("depth", "tile", None),
            P(),
            P(),
        ),
        out_specs=(P(None, "depth", "tile", None), P(None, "tile", "depth")),
        check_vma=False,
    )
```

profile of v0, /device:TPU:0, one launch (start us, length us, event | category | flops | bytes accessed | tf_op | source)
XLA Modules:
  0.0 125.3 jit_solution(16690774001178542910)
XLA Ops:
  4.0 3.7 %collective-permute-start.3 = (f32[8,3,16,128]{3,2,1,0:T(8,128)}, f32[8,3,16,128]{3,2,1,0:T(8,128)}, u32[]{:S(2)}, u32[]{:S(2)}) collective-permute-start(f32[8,3,16,128]{3,2,1,0:T(8,128)} %get-tuple-element.272), channel_id=1, source_target_pairs={{0,1},{1,2},{2,3},{4,5},{5,6},{6,7},{8,9},{9,10},{10,11},{12,13},{... | collective-permute-start | bytes 589832 | tf_op jit(solution)/shard_map/ppermute | solution.py:30
  8.7 6.0 %collective-permute-start.2 = (f32[8,16,3,128]{3,2,1,0:T(4,128)}, f32[8,16,3,128]{3,2,1,0:T(4,128)}, u32[]{:S(2)}, u32[]{:S(2)}) collective-permute-start(f32[8,16,3,128]{3,2,1,0:T(4,128)} %get-tuple-element.267), channel_id=1, source_target_pairs={{4,0},{8,4},{12,8},{16,12},{20,16},{24,20},{28,24},{0,28},{5,1},{9... | collective-permute-start | bytes 589832 | tf_op jit(solution)/shard_map/ppermute | solution.py:32
  17.6 2.2 %pad_maximum_fusion = f32[8,16,16,134]{3,2,1,0:T(8,128)} fusion(f32[8,16,16,3]{3,2,1,0:T(8,128)S(1)} %get-tuple-element.269, f32[1,16,16,128]{3,2,1,0:T(8,128)S(1)} %bitcast.163, f32[3,16,16,128]{3,2,1,0:T(8,128)S(1)} %copy-done.1, f32[3,16,16,128]{3,2,1,0:T(8,128)S(1)} %copy-done, f32[1,16,16,128]{3,2,1,0:T(8,128)S(1)} %bitcast.149, ...), kind=kLoop, calls=%fused_computation.23 | loop fusion | flops 1372160 | bytes 2195456 | tf_op jit(solution)/shard_map/jit(_pad)/concatenate | solution.py:151
  20.4 3.5 %multiply_reduce_fusion.3 = (f32[16,16,134]{2,1,0:T(8,128)}, f32[16,16,134]{2,1,0:T(8,128)}, f32[16,16,134]{2,1,0:T(8,128)}, f32[3,16,16,134]{3,2,1,0:T(8,128)}) fusion(f32[8,16,16,134]{3,2,1,0:T(8,128)} %pad_maximum_fusion, f32[16,16,134]{2,1,0:T(8,128)} %get-tuple-element.251), kind=kLoop, calls=%fused_computation.84 | loop fusion | flops 617472 | bytes 1783808 | tf_op jit(solution)/shard_map/reduce_sum | solution.py:56
  23.9 1.7 %slice_bitcast_fusion = f32[16,16,134]{2,1,0:T(8,128)} fusion(f32[3,16,16,134]{3,2,1,0:T(8,128)} %get-tuple-element.243), kind=kLoop, calls=%fused_computation.116 | loop fusion | bytes 274432 | tf_op jit(solution)/shard_map/mul | solution.py:60
  25.8 2.1 %multiply_subtract_fusion = (f32[3,16,16,134]{3,2,1,0:T(8,128)S(1)}, f32[3,16,16,134]{3,2,1,0:T(8,128)S(1)}) fusion(f32[3,16,16,134]{3,2,1,0:T(8,128)} %get-tuple-element.243, f32[8,16,16,134]{3,2,1,0:T(8,128)} %pad_maximum_fusion, f32[16,16,134]{2,1,0:T(8,128)} %bitcast.178, f32[16,16,134]{2,1,0:T(8,128)} %slice_bitcast_fusion), kind=kLoop, calls=%fused_computation.82 | loop fusion | flops 617472 | bytes 2332672 | tf_op jit(solution)/shard_map/sub | solution.py:61
  37.5 1.6 %fusion.33 = f32[8,16,16,128]{3,2,1,0:T(8,128)S(1)} fusion(f32[8,22,16,128]{3,2,1,0:T(8,128)S(1)} %fusion.24, f32[8,16,16,134]{3,2,1,0:T(8,128)S(1)} %fusion.6, f32[8,16,22,128]{3,2,1,0:T(8,128)S(1)} %fusion.15), kind=kLoop, calls=%fused_computation.55 | loop fusion | flops 6553600 | bytes 19922944 | tf_op jit(solution)/shard_map/neg | solution.py:68
  40.3 53.6 %while.23 = (s32[]{:T(128)}, f32[16,3,16,128]{3,2,1,0:T(8,128)S(1)}, f32[16,3,16,128]{3,2,1,0:T(8,128)S(1)}, f32[16,3,16,128]{3,2,1,0:T(8,128)S(1)}, s32[16]{0:T(128)S(1)}, /*index=5*/s32[]{:T(128)}, s32[]{:T(128)}) while((s32[]{:T(128)}, f32[16,3,16,128]{3,2,1,0:T(8,128)S(1)}, f32[16,3,16,128]{3,2,1,0:T(8,128)S(1)}, ...), condition=%wide.region_12.13_spmd.clone, body=%wide.region_11.12_spmd.clone.sunk | while | flops 294963 | bytes 4325643 | solution.py:103
  40.3 4.8 %collective-permute-start = (f32[16,3,16,128]{3,2,1,0:T(8,128)S(1)}, f32[16,3,16,128]{3,2,1,0:T(8,128)S(1)}, u32[]{:S(2)}, u32[]{:S(2)}) collective-permute-start(f32[16,3,16,128]{3,2,1,0:T(8,128)S(1)} %get-tuple-element.331), channel_id=1, source_target_pairs={{4,0},{8,4},{12,8},{16,12},{20,16},{24,20},{28,24},{0,28},{5,1},{9... | collective-permute-start | bytes 1179656 | tf_op jit(solution)/shard_map/while/body/eval_jaxpr/ppermute | solution.py:19
  45.1 9.4 %collective-permute-done = f32[16,3,16,128]{3,2,1,0:T(8,128)S(1)} collective-permute-done((f32[16,3,16,128]{3,2,1,0:T(8,128)S(1)}, f32[16,3,16,128]{3,2,1,0:T(8,128)S(1)}, u32[]{:S(2)}, u32[]{:S(2)}) %collective-permute-start) | collective-permute-done | bytes 393248 | tf_op jit(solution)/shard_map/while/body/eval_jaxpr/ppermute | solution.py:19
  54.7 5.2 %collective-permute-start = (f32[16,3,16,128]{3,2,1,0:T(8,128)S(1)}, f32[16,3,16,128]{3,2,1,0:T(8,128)S(1)}, u32[]{:S(2)}, u32[]{:S(2)}) collective-permute-start(f32[16,3,16,128]{3,2,1,0:T(8,128)S(1)} %get-tuple-element.331), channel_id=1, source_target_pairs={{4,0},{8,4},{12,8},{16,12},{20,16},{24,20},{28,24},{0,28},{5,1},{9... | collective-permute-start | bytes 1179656 | tf_op jit(solution)/shard_map/while/body/eval_jaxpr/ppermute | solution.py:19
  59.9 8.5 %collective-permute-done = f32[16,3,16,128]{3,2,1,0:T(8,128)S(1)} collective-permute-done((f32[16,3,16,128]{3,2,1,0:T(8,128)S(1)}, f32[16,3,16,128]{3,2,1,0:T(8,128)S(1)}, u32[]{:S(2)}, u32[]{:S(2)}) %collective-permute-start) | collective-permute-done | bytes 393248 | tf_op jit(solution)/shard_map/while/body/eval_jaxpr/ppermute | solution.py:19
  68.7 5.2 %collective-permute-start = (f32[16,3,16,128]{3,2,1,0:T(8,128)S(1)}, f32[16,3,16,128]{3,2,1,0:T(8,128)S(1)}, u32[]{:S(2)}, u32[]{:S(2)}) collective-permute-start(f32[16,3,16,128]{3,2,1,0:T(8,128)S(1)} %get-tuple-element.331), channel_id=1, source_target_pairs={{4,0},{8,4},{12,8},{16,12},{20,16},{24,20},{28,24},{0,28},{5,1},{9... | collective-permute-start | bytes 1179656 | tf_op jit(solution)/shard_map/while/body/eval_jaxpr/ppermute | solution.py:19
  73.9 7.6 %collective-permute-done = f32[16,3,16,128]{3,2,1,0:T(8,128)S(1)} collective-permute-done((f32[16,3,16,128]{3,2,1,0:T(8,128)S(1)}, f32[16,3,16,128]{3,2,1,0:T(8,128)S(1)}, u32[]{:S(2)}, u32[]{:S(2)}) %collective-permute-start) | collective-permute-done | bytes 393248 | tf_op jit(solution)/shard_map/while/body/eval_jaxpr/ppermute | solution.py:19
  81.7 5.2 %collective-permute-start = (f32[16,3,16,128]{3,2,1,0:T(8,128)S(1)}, f32[16,3,16,128]{3,2,1,0:T(8,128)S(1)}, u32[]{:S(2)}, u32[]{:S(2)}) collective-permute-start(f32[16,3,16,128]{3,2,1,0:T(8,128)S(1)} %get-tuple-element.331), channel_id=1, source_target_pairs={{4,0},{8,4},{12,8},{16,12},{20,16},{24,20},{28,24},{0,28},{5,1},{9... | collective-permute-start | bytes 1179656 | tf_op jit(solution)/shard_map/while/body/eval_jaxpr/ppermute | solution.py:19
  87.0 6.8 %collective-permute-done = f32[16,3,16,128]{3,2,1,0:T(8,128)S(1)} collective-permute-done((f32[16,3,16,128]{3,2,1,0:T(8,128)S(1)}, f32[16,3,16,128]{3,2,1,0:T(8,128)S(1)}, u32[]{:S(2)}, u32[]{:S(2)}) %collective-permute-start) | collective-permute-done | bytes 393248 | tf_op jit(solution)/shard_map/while/body/eval_jaxpr/ppermute | solution.py:19
  95.2 2.1 %copy.37 = f32[16,3,16,128]{2,0,1,3:T(8,128)S(1)} copy(f32[16,3,16,128]{3,2,1,0:T(8,128)} %convolution_bitcast_fusion.1) | data formatting | bytes 786432 | tf_op jit(solution)/shard_map/lcxa,lwx->lcwa/transpose | solution.py:112
  97.2 1.8 %reshape.515 = f32[4,1,24576]{2,1,0:T(1,128)} reshape(f32[128,3,16,16]{3,2,1,0:T(8,128)S(1)} %bitcast.175) | data formatting | bytes 786432
  99.1 3.6 %all-to-all-start = ((f32[4,1,24576]{2,1,0:T(1,128)}), f32[4,1,24576]{2,1,0:T(1,128)S(1)}, u32[]{:S(2)}, u32[]{:S(2)}) async-start(f32[4,1,24576]{2,1,0:T(1,128)} %reshape.515), calls=%async_computation | async-start | bytes 786432 | tf_op jit(solution)/shard_map/all_to_all | solution.py:116
  102.8 7.2 %all-to-all-done = f32[4,1,24576]{2,1,0:T(1,128)S(1)} async-done(((f32[4,1,24576]{2,1,0:T(1,128)}), f32[4,1,24576]{2,1,0:T(1,128)S(1)}, u32[]{:S(2)}, u32[]{:S(2)}) %all-to-all-start) | async-done | bytes 393248 | tf_op jit(solution)/shard_map/all_to_all | solution.py:116
  110.4 1.8 %reduce.16 = f32[4,24576]{1,0:T(4,128)S(1)} reduce(f32[4,1,24576]{2,1,0:T(1,128)S(1)} %all-to-all-done, f32[]{:T(128)} %broadcast.492), dimensions={1}, to_apply=%all_to_all.13.reduce_sub_computation | reduce | bytes 786436 | tf_op jit(solution)/shard_map/all_to_all | solution.py:116
  113.3 2.2 %copy.38 = f32[16,3,16,4,32]{4,2,1,0,3:T(8,128)} copy(f32[16,3,16,4,32]{2,0,1,4,3:T(8,128)S(1)} %bitcast.176) | data formatting | bytes 786432 | tf_op jit(solution)/shard_map/all_to_all | solution.py:116
  115.6 2.0 %gather_fusion = f32[24,3,16,32]{3,2,1,0:T(8,128)S(1)} fusion(f32[64,3,16,32]{3,2,1,0:T(8,128)} %bitcast.177, s32[1024]{0:T(1024)S(1)} %pad_clamp_fusion), kind=kCustom, calls=%fused_computation | custom fusion | bytes 295008 | tf_op jit(solution)/shard_map/gather | solution.py:160
  118.0 4.4 %fusion.3 = (f32[48,24,512]{2,1,0:T(8,128)S(1)}, f32[48,512]{1,0:T(8,128)S(1)}, f32[48,24,512]{2,1,0:T(8,128)}) fusion(f32[24,512]{1,0:T(8,128)S(1)} %get-tuple-element.282, f32[48]{0:T(128)S(1)} %copy-done.13, f32[24,512]{1,0:T(8,128)S(1)} %get-tuple-element.283, f32[24,512]{1,0:T(8,128)S(1)} %bitcast.181), kind=kOutput, calls=%fused_computation.9 | convolution fusion | flops 180462144 | bytes 4964544 | tf_op jit(solution)/shard_map/kj,wjc->wkc/dot_general | solution.py:130
  (104 shorter events, 25.5 us)
Async XLA Ops:
  2.7 27.7 %collective-permute-start.4 = (f32[8,3,16,128]{3,2,1,0:T(8,128)}, f32[8,3,16,128]{3,2,1,0:T(8,128)}, u32[]{:S(2)}, u32[]{:S(2)}) collective-permute-start(f32[8,3,16,128]{3,2,1,0:T(8,128)} %get-tuple-element.273), channel_id=1, source_target_pairs={{1,0},{2,1},{3,2},{5,4},{6,5},{7,6},{9,8},{10,9},{11,10},{13,12},{... | collective-permute-start | bytes 589832 | tf_op jit(solution)/shard_map/ppermute | solution.py:32
  4.0 27.9 %collective-permute-start.3 = (f32[8,3,16,128]{3,2,1,0:T(8,128)}, f32[8,3,16,128]{3,2,1,0:T(8,128)}, u32[]{:S(2)}, u32[]{:S(2)}) collective-permute-start(f32[8,3,16,128]{3,2,1,0:T(8,128)} %get-tuple-element.272), channel_id=1, source_target_pairs={{0,1},{1,2},{2,3},{4,5},{5,6},{6,7},{8,9},{9,10},{10,11},{12,13},{... | collective-permute-start | bytes 589832 | tf_op jit(solution)/shard_map/ppermute | solution.py:30
  8.7 23.6 %collective-permute-start.2 = (f32[8,16,3,128]{3,2,1,0:T(4,128)}, f32[8,16,3,128]{3,2,1,0:T(4,128)}, u32[]{:S(2)}, u32[]{:S(2)}) collective-permute-start(f32[8,16,3,128]{3,2,1,0:T(4,128)} %get-tuple-element.267), channel_id=1, source_target_pairs={{4,0},{8,4},{12,8},{16,12},{20,16},{24,20},{28,24},{0,28},{5,1},{9... | collective-permute-start | bytes 589832 | tf_op jit(solution)/shard_map/ppermute | solution.py:32
  14.7 17.7 %collective-permute-start.1 = (f32[8,16,3,128]{3,2,1,0:T(4,128)}, f32[8,16,3,128]{3,2,1,0:T(4,128)}, u32[]{:S(2)}, u32[]{:S(2)}) collective-permute-start(f32[8,16,3,128]{3,2,1,0:T(4,128)} %get-tuple-element.266), channel_id=1, source_target_pairs={{0,4},{4,8},{8,12},{12,16},{16,20},{20,24},{24,28},{28,0},{1,5},{5... | collective-permute-start | bytes 589832 | tf_op jit(solution)/shard_map/ppermute | solution.py:30
  15.3 1.0 copy-start
  15.3 1.1 copy-start.1
  15.3 1.1 copy-start.2
  15.3 1.2 copy-start.3
  20.4 5.2 %copy-start.11 = (s32[24]{0:T(128)S(1)}, s32[24]{0:T(128)}, u32[]{:S(2)}) copy-start(s32[24]{0:T(128)} %param.22) | copy-start | bytes 292
  20.4 5.2 %copy-start.12 = (s32[24]{0:T(128)S(1)}, s32[24]{0:T(128)}, u32[]{:S(2)}) copy-start(s32[24]{0:T(128)} %param.23) | copy-start | bytes 292
  25.8 2.1 %copy-start.6 = (f32[16,16,134]{2,1,0:T(8,128)S(1)}, f32[16,16,134]{2,1,0:T(8,128)}, u32[]{:S(2)}) copy-start(f32[16,16,134]{2,1,0:T(8,128)} %get-tuple-element.217) | copy-start | bytes 411652
  25.8 2.2 %copy-start.7 = (f32[16,16,134]{2,1,0:T(8,128)S(1)}, f32[16,16,134]{2,1,0:T(8,128)}, u32[]{:S(2)}) copy-start(f32[16,16,134]{2,1,0:T(8,128)} %get-tuple-element.221) | copy-start | bytes 411652
  28.0 1.0 copy-start.5
  28.0 1.0 copy-start.8
  30.1 0.8 copy-start.10
  30.1 1.8 %copy-start.9 = (f32[8,16,128]{2,1,0:T(8,128)S(1)}, f32[8,16,128]{2,1,0:T(8,128)}, u32[]{:S(2)}) copy-start(f32[8,16,128]{2,1,0:T(8,128)} %get-tuple-element.270) | copy-start | bytes 196612
  39.3 1.0 copy-start.4
  40.3 14.1 %collective-permute-start = (f32[16,3,16,128]{3,2,1,0:T(8,128)S(1)}, f32[16,3,16,128]{3,2,1,0:T(8,128)S(1)}, u32[]{:S(2)}, u32[]{:S(2)}) collective-permute-start(f32[16,3,16,128]{3,2,1,0:T(8,128)S(1)} %get-tuple-element.331), channel_id=1, source_target_pairs={{4,0},{8,4},{12,8},{16,12},{20,16},{24,20},{28,24},{0,28},{5,1},{9... | collective-permute-start | bytes 1179656 | tf_op jit(solution)/shard_map/while/body/eval_jaxpr/ppermute | solution.py:19
  54.7 13.7 %collective-permute-start = (f32[16,3,16,128]{3,2,1,0:T(8,128)S(1)}, f32[16,3,16,128]{3,2,1,0:T(8,128)S(1)}, u32[]{:S(2)}, u32[]{:S(2)}) collective-permute-start(f32[16,3,16,128]{3,2,1,0:T(8,128)S(1)} %get-tuple-element.331), channel_id=1, source_target_pairs={{4,0},{8,4},{12,8},{16,12},{20,16},{24,20},{28,24},{0,28},{5,1},{9... | collective-permute-start | bytes 1179656 | tf_op jit(solution)/shard_map/while/body/eval_jaxpr/ppermute | solution.py:19
  68.7 12.9 %collective-permute-start = (f32[16,3,16,128]{3,2,1,0:T(8,128)S(1)}, f32[16,3,16,128]{3,2,1,0:T(8,128)S(1)}, u32[]{:S(2)}, u32[]{:S(2)}) collective-permute-start(f32[16,3,16,128]{3,2,1,0:T(8,128)S(1)} %get-tuple-element.331), channel_id=1, source_target_pairs={{4,0},{8,4},{12,8},{16,12},{20,16},{24,20},{28,24},{0,28},{5,1},{9... | collective-permute-start | bytes 1179656 | tf_op jit(solution)/shard_map/while/body/eval_jaxpr/ppermute | solution.py:19
  81.7 12.0 %collective-permute-start = (f32[16,3,16,128]{3,2,1,0:T(8,128)S(1)}, f32[16,3,16,128]{3,2,1,0:T(8,128)S(1)}, u32[]{:S(2)}, u32[]{:S(2)}) collective-permute-start(f32[16,3,16,128]{3,2,1,0:T(8,128)S(1)} %get-tuple-element.331), channel_id=1, source_target_pairs={{4,0},{8,4},{12,8},{16,12},{20,16},{24,20},{28,24},{0,28},{5,1},{9... | collective-permute-start | bytes 1179656 | tf_op jit(solution)/shard_map/while/body/eval_jaxpr/ppermute | solution.py:19
  99.1 10.8 %all-to-all-start = ((f32[4,1,24576]{2,1,0:T(1,128)}), f32[4,1,24576]{2,1,0:T(1,128)S(1)}, u32[]{:S(2)}, u32[]{:S(2)}) async-start(f32[4,1,24576]{2,1,0:T(1,128)} %reshape.515), calls=%async_computation | async-start | bytes 786432 | tf_op jit(solution)/shard_map/all_to_all | solution.py:116
  115.6 2.4 %copy-start.13 = (f32[48]{0:T(128)S(1)}, f32[48]{0:T(128)}, u32[]{:S(2)}) copy-start(f32[48]{0:T(128)} %add_multiply_fusion) | copy-start | bytes 580
where the time goes:
time: 126 us; the launch traced here: 125 us
  waiting for transfers between devices  39.5 us (31%)
  starting transfers between devices  35.1 us (28%)
  other arithmetic  25.2 us (20%)
  local copies, waits for them, and re-layouts  18.8 us (15%)
  matrix products  5.57 us (4%)
    ppermute x4, waiting for transfers between devices, shifted(): return lax.ppermute(block, axis, route)  32.3 us
    ppermute x4, starting transfers between devices, shifted(): return lax.ppermute(block, axis, route)  20.5 us
    ppermute x2, starting transfers between devices, padded_2(): lax.ppermute(head, axis, [((i + 1) % count, i) for i in range(ends)])  7.28 us
    all_to_all x1, waiting for transfers between devices, regroup(): lax.all_to_all(rows, 'depth', split_axis=3, concat_axis=0, tiled=True)  7.17 us
    unnamed x35, local copies, waits for them, and re-layouts  6.68 us
    dot_general x1, matrix products, emergent(): jnp.einsum('kj,wjc->wkc', earlier, dtau, precision=lax.Precision.HIGHEST)  4.39 us
    reduce_sum x3, other arithmetic, flux(): jnp.sum(moment * velocity, axis=0)  3.84 us
    ppermute x2, starting transfers between devices, padded_2(): lax.ppermute(tail, axis, [(i, (i + 1) % count) for i in range(ends)])  3.72 us
  transfers between devices with their start and end apart: 9, of which 5 were waited for; matrix products, arithmetic and copies ran while one was open for 13% of the time, Pallas kernels for 0%

commit v1 on v0

--- a/solution.py
+++ b/solution.py
@@ -11,6 +11,12 @@
 COS_VIEW = 0.5
 STRENGTH = 4.0
 SPACING = 0.25
+
+
+def exchange_blocks(value, axis, split, join):
+    pieces = jnp.split(value, lax.axis_size(axis), axis=split)
+    received = lax.all_to_all(jnp.stack(pieces), axis, 0, 0)
+    return jnp.concatenate(received, axis=join)
 
 
 def shifted(block, axis, distance):
@@ -113,7 +119,7 @@
 
 
 def regroup(rows):
-    return lax.all_to_all(rows, "depth", split_axis=3, concat_axis=0, tiled=True)
+    return exchange_blocks(rows, "depth", 3, 0)
 
 
 def emergent(columns):

time: 126 us -> 118 us (0.937)
  local copies, waits for them, and re-layouts: 18.8 us -> 12.3 us
    all_to_all x2 -> x1, local copies, waits for them, and re-layouts: 2.75 us -> 0.51 us  [exchange_blocks(): received = lax.all_to_all(jnp.stack(pieces), axis, 0, 0)]
    transpose x1 -> x0, local copies, waits for them, and re-layouts: 2.06 us -> none  [shear(): jnp.einsum('lcxa,lwx->lcwa', joined, select, precision=lax.Precision.HIGH...]
    gather x1, local copies, waits for them, and re-layouts: 1.99 us -> 0.59 us  [per_device(): columns = regroup(shear(fields, level_shift, reach))[levels]]
  transfers between devices with their start and end apart: 9 -> 9, of which waited for: 5 -> 5; matrix products, arithmetic and copies ran while one was open for 13% -> 12% of each run, Pallas kernels for 0% -> 0%
where the time goes in v1:
time: 118 us; the launch traced here: 117 us
  waiting for transfers between devices  39.5 us (33%)
  starting transfers between devices  35.1 us (30%)
  other arithmetic  24 us (20%)
  local copies, waits for them, and re-layouts  12.3 us (10%)
  matrix products  4.83 us (4%)
    ppermute x4, waiting for transfers between devices, shifted(): return lax.ppermute(block, axis, route)  32.3 us
    ppermute x4, starting transfers between devices, shifted(): return lax.ppermute(block, axis, route)  20.5 us
    ppermute x2, starting transfers between devices, padded_2(): lax.ppermute(head, axis, [((i + 1) % count, i) for i in range(ends)])  7.28 us
    all_to_all x1, waiting for transfers between devices, exchange_blocks(): received = lax.all_to_all(jnp.stack(pieces), axis, 0, 0)  7.17 us
    unnamed x35, local copies, waits for them, and re-layouts  6.55 us
    dot_general x1, matrix products, emergent(): jnp.einsum('kj,wjc->wkc', earlier, dtau, precision=lax.Precision.HIGHEST)  4.39 us
    ppermute x2, starting transfers between devices, padded_2(): lax.ppermute(tail, axis, [(i, (i + 1) % count) for i in range(ends)])  3.72 us
    all_to_all x1, starting transfers between devices, exchange_blocks(): received = lax.all_to_all(jnp.stack(pieces), axis, 0, 0)  3.64 us
  transfers between devices with their start and end apart: 9, of which 5 were waited for; matrix products, arithmetic and copies ran while one was open for 12% of the time, Pallas kernels for 0%

profile of v1, /device:TPU:0, one launch (start us, length us, event | category | flops | bytes accessed | tf_op | source)
XLA Modules:
  0.0 116.9 jit_solution(11248257557321033254)
XLA Ops:
  0.6 1.3 %pad_maximum_fusion.5 = f32[8,16,16,128]{3,2,1,0:T(8,128)S(1)} fusion(f32[1,16,16,128]{3,2,1,0:T(8,128)} %bitcast.164, f32[3,16,16,128]{3,2,1,0:T(8,128)} %param.20, f32[3,16,16,128]{3,2,1,0:T(8,128)} %param.19, f32[1,16,16,128]{3,2,1,0:T(8,128)} %bitcast.150), kind=kLoop, calls=%fused_computation.77 | loop fusion | flops 786432 | bytes 2097152 | tf_op jit(solution)/shard_map/concatenate | solution.py:143
  2.7 1.3 %collective-permute-start.4 = (f32[8,3,16,128]{3,2,1,0:T(8,128)}, f32[8,3,16,128]{3,2,1,0:T(8,128)}, u32[]{:S(2)}, u32[]{:S(2)}) collective-permute-start(f32[8,3,16,128]{3,2,1,0:T(8,128)} %get-tuple-element.259), channel_id=1, source_target_pairs={{1,0},{2,1},{3,2},{5,4},{6,5},{7,6},{9,8},{10,9},{11,10},{13,12},{... | collective-permute-start | bytes 589832 | tf_op jit(solution)/shard_map/ppermute | solution.py:38
  4.0 3.7 %collective-permute-start.3 = (f32[8,3,16,128]{3,2,1,0:T(8,128)}, f32[8,3,16,128]{3,2,1,0:T(8,128)}, u32[]{:S(2)}, u32[]{:S(2)}) collective-permute-start(f32[8,3,16,128]{3,2,1,0:T(8,128)} %get-tuple-element.258), channel_id=1, source_target_pairs={{0,1},{1,2},{2,3},{4,5},{5,6},{6,7},{8,9},{9,10},{10,11},{12,13},{... | collective-permute-start | bytes 589832 | tf_op jit(solution)/shard_map/ppermute | solution.py:36
  8.6 6.0 %collective-permute-start.2 = (f32[8,16,3,128]{3,2,1,0:T(4,128)}, f32[8,16,3,128]{3,2,1,0:T(4,128)}, u32[]{:S(2)}, u32[]{:S(2)}) collective-permute-start(f32[8,16,3,128]{3,2,1,0:T(4,128)} %get-tuple-element.253), channel_id=1, source_target_pairs={{4,0},{8,4},{12,8},{16,12},{20,16},{24,20},{28,24},{0,28},{5,1},{9... | collective-permute-start | bytes 589832 | tf_op jit(solution)/shard_map/ppermute | solution.py:38
  17.6 2.2 %pad_maximum_fusion = f32[8,16,16,134]{3,2,1,0:T(8,128)} fusion(f32[8,16,16,3]{3,2,1,0:T(8,128)S(1)} %get-tuple-element.255, f32[1,16,16,128]{3,2,1,0:T(8,128)S(1)} %bitcast.166, f32[3,16,16,128]{3,2,1,0:T(8,128)S(1)} %copy-done.1, f32[3,16,16,128]{3,2,1,0:T(8,128)S(1)} %copy-done, f32[1,16,16,128]{3,2,1,0:T(8,128)S(1)} %bitcast.152, ...), kind=kLoop, calls=%fused_computation.23 | loop fusion | flops 1372160 | bytes 2195456 | tf_op jit(solution)/shard_map/jit(_pad)/concatenate | solution.py:157
  19.8 2.7 %multiply_reduce_fusion.3 = (f32[16,16,134]{2,1,0:T(8,128)}, f32[16,16,134]{2,1,0:T(8,128)}, f32[16,16,134]{2,1,0:T(8,128)}, f32[3,16,16,134]{3,2,1,0:T(8,128)S(1)}) fusion(f32[8,16,16,134]{3,2,1,0:T(8,128)} %pad_maximum_fusion, f32[16,16,134]{2,1,0:T(8,128)} %get-tuple-element.237), kind=kLoop, calls=%fused_computation.85 | loop fusion | flops 617472 | bytes 1783808 | tf_op jit(solution)/shard_map/reduce_sum | solution.py:62
  24.4 2.1 %multiply_subtract_fusion = (f32[3,16,16,134]{3,2,1,0:T(8,128)S(1)}, f32[3,16,16,134]{3,2,1,0:T(8,128)S(1)}) fusion(f32[3,16,16,134]{3,2,1,0:T(8,128)} %copy-done.4, f32[8,16,16,134]{3,2,1,0:T(8,128)} %pad_maximum_fusion, f32[16,16,134]{2,1,0:T(8,128)} %bitcast.179, f32[16,16,134]{2,1,0:T(8,128)} %slice_bitcast_fusion.4), kind=kLoop, calls=%fused_computation.83 | loop fusion | flops 617472 | bytes 2332672 | tf_op jit(solution)/shard_map/sub | solution.py:67
  31.8 1.3 %pad_maximum_fusion.1 = f32[8,16,22,128]{3,2,1,0:T(8,128)S(1)} fusion(f32[8,16,3,128]{3,2,1,0:T(4,128)} %collective-permute-done.2, f32[1,16,16,128]{3,2,1,0:T(8,128)S(1)} %bitcast.172, f32[3,16,16,128]{3,2,1,0:T(8,128)S(1)} %copy-done.1, f32[3,16,16,128]{3,2,1,0:T(8,128)S(1)} %copy-done, f32[1,16,16,128]{3,2,1,0:T(8,128)S(1)} %bitcast.158, ...), kind=kLoop, calls=%fused_computation.37 | loop fusion | flops 1802240 | bytes 2883584 | tf_op jit(solution)/shard_map/concatenate | solution.py:34
  36.1 1.6 %fusion.33 = f32[8,16,16,128]{3,2,1,0:T(8,128)S(1)} fusion(f32[8,22,16,128]{3,2,1,0:T(8,128)S(1)} %fusion.24, f32[8,16,16,134]{3,2,1,0:T(8,128)S(1)} %fusion.6, f32[8,16,22,128]{3,2,1,0:T(8,128)S(1)} %fusion.15), kind=kLoop, calls=%fused_computation.56 | loop fusion | flops 6553600 | bytes 19922944 | tf_op jit(solution)/shard_map/neg | solution.py:74
  38.9 53.6 %while.23 = (s32[]{:T(128)}, f32[16,3,16,128]{3,2,1,0:T(8,128)S(1)}, f32[16,3,16,128]{3,2,1,0:T(8,128)S(1)}, f32[16,3,16,128]{3,2,1,0:T(8,128)S(1)}, s32[16]{0:T(128)S(1)}, /*index=5*/s32[]{:T(128)}, s32[]{:T(128)}) while((s32[]{:T(128)}, f32[16,3,16,128]{3,2,1,0:T(8,128)S(1)}, f32[16,3,16,128]{3,2,1,0:T(8,128)S(1)}, ...), condition=%wide.region_12.13_spmd.clone, body=%wide.region_11.12_spmd.clone.sunk | while | flops 294963 | bytes 4325643 | solution.py:109
  38.9 4.8 %collective-permute-start = (f32[16,3,16,128]{3,2,1,0:T(8,128)S(1)}, f32[16,3,16,128]{3,2,1,0:T(8,128)S(1)}, u32[]{:S(2)}, u32[]{:S(2)}) collective-permute-start(f32[16,3,16,128]{3,2,1,0:T(8,128)S(1)} %get-tuple-element.321), channel_id=1, source_target_pairs={{4,0},{8,4},{12,8},{16,12},{20,16},{24,20},{28,24},{0,28},{5,1},{9... | collective-permute-start | bytes 1179656 | tf_op jit(solution)/shard_map/while/body/eval_jaxpr/ppermute | solution.py:25
  43.7 9.4 %collective-permute-done = f32[16,3,16,128]{3,2,1,0:T(8,128)S(1)} collective-permute-done((f32[16,3,16,128]{3,2,1,0:T(8,128)S(1)}, f32[16,3,16,128]{3,2,1,0:T(8,128)S(1)}, u32[]{:S(2)}, u32[]{:S(2)}) %collective-permute-start) | collective-permute-done | bytes 393248 | tf_op jit(solution)/shard_map/while/body/eval_jaxpr/ppermute | solution.py:25
  53.3 5.2 %collective-permute-start = (f32[16,3,16,128]{3,2,1,0:T(8,128)S(1)}, f32[16,3,16,128]{3,2,1,0:T(8,128)S(1)}, u32[]{:S(2)}, u32[]{:S(2)}) collective-permute-start(f32[16,3,16,128]{3,2,1,0:T(8,128)S(1)} %get-tuple-element.321), channel_id=1, source_target_pairs={{4,0},{8,4},{12,8},{16,12},{20,16},{24,20},{28,24},{0,28},{5,1},{9... | collective-permute-start | bytes 1179656 | tf_op jit(solution)/shard_map/while/body/eval_jaxpr/ppermute | solution.py:25
  58.5 8.5 %collective-permute-done = f32[16,3,16,128]{3,2,1,0:T(8,128)S(1)} collective-permute-done((f32[16,3,16,128]{3,2,1,0:T(8,128)S(1)}, f32[16,3,16,128]{3,2,1,0:T(8,128)S(1)}, u32[]{:S(2)}, u32[]{:S(2)}) %collective-permute-start) | collective-permute-done | bytes 393248 | tf_op jit(solution)/shard_map/while/body/eval_jaxpr/ppermute | solution.py:25
  67.2 5.2 %collective-permute-start = (f32[16,3,16,128]{3,2,1,0:T(8,128)S(1)}, f32[16,3,16,128]{3,2,1,0:T(8,128)S(1)}, u32[]{:S(2)}, u32[]{:S(2)}) collective-permute-start(f32[16,3,16,128]{3,2,1,0:T(8,128)S(1)} %get-tuple-element.321), channel_id=1, source_target_pairs={{4,0},{8,4},{12,8},{16,12},{20,16},{24,20},{28,24},{0,28},{5,1},{9... | collective-permute-start | bytes 1179656 | tf_op jit(solution)/shard_map/while/body/eval_jaxpr/ppermute | solution.py:25
  72.5 7.6 %collective-permute-done = f32[16,3,16,128]{3,2,1,0:T(8,128)S(1)} collective-permute-done((f32[16,3,16,128]{3,2,1,0:T(8,128)S(1)}, f32[16,3,16,128]{3,2,1,0:T(8,128)S(1)}, u32[]{:S(2)}, u32[]{:S(2)}) %collective-permute-start) | collective-permute-done | bytes 393248 | tf_op jit(solution)/shard_map/while/body/eval_jaxpr/ppermute | solution.py:25
  80.3 5.2 %collective-permute-start = (f32[16,3,16,128]{3,2,1,0:T(8,128)S(1)}, f32[16,3,16,128]{3,2,1,0:T(8,128)S(1)}, u32[]{:S(2)}, u32[]{:S(2)}) collective-permute-start(f32[16,3,16,128]{3,2,1,0:T(8,128)S(1)} %get-tuple-element.321), channel_id=1, source_target_pairs={{4,0},{8,4},{12,8},{16,12},{20,16},{24,20},{28,24},{0,28},{5,1},{9... | collective-permute-start | bytes 1179656 | tf_op jit(solution)/shard_map/while/body/eval_jaxpr/ppermute | solution.py:25
  85.5 6.8 %collective-permute-done = f32[16,3,16,128]{3,2,1,0:T(8,128)S(1)} collective-permute-done((f32[16,3,16,128]{3,2,1,0:T(8,128)S(1)}, f32[16,3,16,128]{3,2,1,0:T(8,128)S(1)}, u32[]{:S(2)}, u32[]{:S(2)}) %collective-permute-start) | collective-permute-done | bytes 393248 | tf_op jit(solution)/shard_map/while/body/eval_jaxpr/ppermute | solution.py:25
  93.5 1.4 %reshape.519 = f32[4,1,24576]{2,1,0:T(1,128)} reshape(f32[4,16,3,16,32]{4,3,2,1,0:T(8,128)S(1)} %pad_maximum_fusion.2) | data formatting | bytes 786432
  95.0 3.6 %all-to-all-start = ((f32[4,1,24576]{2,1,0:T(1,128)}), f32[4,1,24576]{2,1,0:T(1,128)S(1)}, u32[]{:S(2)}, u32[]{:S(2)}) async-start(f32[4,1,24576]{2,1,0:T(1,128)} %reshape.519), calls=%async_computation | async-start | bytes 786432 | tf_op jit(solution)/shard_map/all_to_all | solution.py:18
  98.6 7.2 %all-to-all-done = f32[4,1,24576]{2,1,0:T(1,128)S(1)} async-done(((f32[4,1,24576]{2,1,0:T(1,128)}), f32[4,1,24576]{2,1,0:T(1,128)S(1)}, u32[]{:S(2)}, u32[]{:S(2)}) %all-to-all-start) | async-done | bytes 393248 | tf_op jit(solution)/shard_map/all_to_all | solution.py:18
  106.3 1.8 %reduce.16 = f32[4,24576]{1,0:T(4,128)S(1)} reduce(f32[4,1,24576]{2,1,0:T(1,128)S(1)} %all-to-all-done, f32[]{:T(128)} %broadcast.492), dimensions={1}, to_apply=%all_to_all.3.reduce_sub_computation | reduce | bytes 786436 | tf_op jit(solution)/shard_map/all_to_all | solution.py:18
  109.6 4.4 %fusion.3 = (f32[48,24,512]{2,1,0:T(8,128)S(1)}, f32[48,512]{1,0:T(8,128)S(1)}, f32[48,24,512]{2,1,0:T(8,128)}) fusion(f32[24,512]{1,0:T(8,128)S(1)} %get-tuple-element.272, f32[48]{0:T(128)S(1)} %add_multiply_fusion, f32[24,512]{1,0:T(8,128)S(1)} %get-tuple-element.273, f32[24,512]{1,0:T(8,128)S(1)} %bitcast.182), kind=kOutput, calls=%fused_computation.9 | convolution fusion | flops 180462144 | bytes 4964544 | tf_op jit(solution)/shard_map/kj,wjc->wkc/dot_general | solution.py:136
  114.2 1.6 %fusion.70 = f32[48,512]{1,0:T(8,128)S(1)} fusion(f32[48,24,512]{2,1,0:T(8,128)S(1)} %get-tuple-element.269, f32[48,24,512]{2,1,0:T(8,128)} %get-tuple-element.271), kind=kLoop, calls=%fused_computation.168 | loop fusion | flops 49152 | bytes 294912 | tf_op jit(solution)/shard_map/exp | solution.py:138
  (104 shorter events, 20.9 us)
Async XLA Ops:
  2.7 26.3 %collective-permute-start.4 = (f32[8,3,16,128]{3,2,1,0:T(8,128)}, f32[8,3,16,128]{3,2,1,0:T(8,128)}, u32[]{:S(2)}, u32[]{:S(2)}) collective-permute-start(f32[8,3,16,128]{3,2,1,0:T(8,128)} %get-tuple-element.259), channel_id=1, source_target_pairs={{1,0},{2,1},{3,2},{5,4},{6,5},{7,6},{9,8},{10,9},{11,10},{13,12},{... | collective-permute-start | bytes 589832 | tf_op jit(solution)/shard_map/ppermute | solution.py:38
  4.0 26.5 %collective-permute-start.3 = (f32[8,3,16,128]{3,2,1,0:T(8,128)}, f32[8,3,16,128]{3,2,1,0:T(8,128)}, u32[]{:S(2)}, u32[]{:S(2)}) collective-permute-start(f32[8,3,16,128]{3,2,1,0:T(8,128)} %get-tuple-element.258), channel_id=1, source_target_pairs={{0,1},{1,2},{2,3},{4,5},{5,6},{6,7},{8,9},{9,10},{10,11},{12,13},{... | collective-permute-start | bytes 589832 | tf_op jit(solution)/shard_map/ppermute | solution.py:36
  8.6 22.2 %collective-permute-start.2 = (f32[8,16,3,128]{3,2,1,0:T(4,128)}, f32[8,16,3,128]{3,2,1,0:T(4,128)}, u32[]{:S(2)}, u32[]{:S(2)}) collective-permute-start(f32[8,16,3,128]{3,2,1,0:T(4,128)} %get-tuple-element.253), channel_id=1, source_target_pairs={{4,0},{8,4},{12,8},{16,12},{20,16},{24,20},{28,24},{0,28},{5,1},{9... | collective-permute-start | bytes 589832 | tf_op jit(solution)/shard_map/ppermute | solution.py:38
  14.7 16.2 %collective-permute-start.1 = (f32[8,16,3,128]{3,2,1,0:T(4,128)}, f32[8,16,3,128]{3,2,1,0:T(4,128)}, u32[]{:S(2)}, u32[]{:S(2)}) collective-permute-start(f32[8,16,3,128]{3,2,1,0:T(4,128)} %get-tuple-element.252), channel_id=1, source_target_pairs={{0,4},{4,8},{8,12},{12,16},{16,20},{20,24},{24,28},{28,0},{1,5},{5... | collective-permute-start | bytes 589832 | tf_op jit(solution)/shard_map/ppermute | solution.py:36
  15.3 1.0 copy-start
  15.3 1.1 copy-start.1
  15.3 1.1 copy-start.2
  15.3 1.2 %copy-start.3 = (f32[16,16,128]{2,1,0:T(8,128)S(1)}, f32[16,16,128]{2,1,0:T(8,128)}, u32[]{:S(2)}) copy-start(f32[16,16,128]{2,1,0:T(8,128)} %param.21) | copy-start | bytes 393220
  19.8 4.3 %copy-start.12 = (s32[24]{0:T(128)S(1)}, s32[24]{0:T(128)}, u32[]{:S(2)}) copy-start(s32[24]{0:T(128)} %param.22) | copy-start | bytes 292
  19.8 4.3 %copy-start.13 = (s32[24]{0:T(128)S(1)}, s32[24]{0:T(128)}, u32[]{:S(2)}) copy-start(s32[24]{0:T(128)} %param.23) | copy-start | bytes 292
  22.5 0.9 copy-start.4
  24.4 2.1 %copy-start.7 = (f32[16,16,134]{2,1,0:T(8,128)S(1)}, f32[16,16,134]{2,1,0:T(8,128)}, u32[]{:S(2)}) copy-start(f32[16,16,134]{2,1,0:T(8,128)} %get-tuple-element.203) | copy-start | bytes 411652
  24.4 2.2 %copy-start.8 = (f32[16,16,134]{2,1,0:T(8,128)S(1)}, f32[16,16,134]{2,1,0:T(8,128)}, u32[]{:S(2)}) copy-start(f32[16,16,134]{2,1,0:T(8,128)} %get-tuple-element.207) | copy-start | bytes 411652
  26.5 1.0 copy-start.6
  26.5 1.0 copy-start.9
  28.7 0.8 copy-start.11
  28.7 1.8 %copy-start.10 = (f32[8,16,128]{2,1,0:T(8,128)S(1)}, f32[8,16,128]{2,1,0:T(8,128)}, u32[]{:S(2)}) copy-start(f32[8,16,128]{2,1,0:T(8,128)} %get-tuple-element.256) | copy-start | bytes 196612
  37.9 1.0 copy-start.5
  38.9 14.1 %collective-permute-start = (f32[16,3,16,128]{3,2,1,0:T(8,128)S(1)}, f32[16,3,16,128]{3,2,1,0:T(8,128)S(1)}, u32[]{:S(2)}, u32[]{:S(2)}) collective-permute-start(f32[16,3,16,128]{3,2,1,0:T(8,128)S(1)} %get-tuple-element.321), channel_id=1, source_target_pairs={{4,0},{8,4},{12,8},{16,12},{20,16},{24,20},{28,24},{0,28},{5,1},{9... | collective-permute-start | bytes 1179656 | tf_op jit(solution)/shard_map/while/body/eval_jaxpr/ppermute | solution.py:25
  53.3 13.7 %collective-permute-start = (f32[16,3,16,128]{3,2,1,0:T(8,128)S(1)}, f32[16,3,16,128]{3,2,1,0:T(8,128)S(1)}, u32[]{:S(2)}, u32[]{:S(2)}) collective-permute-start(f32[16,3,16,128]{3,2,1,0:T(8,128)S(1)} %get-tuple-element.321), channel_id=1, source_target_pairs={{4,0},{8,4},{12,8},{16,12},{20,16},{24,20},{28,24},{0,28},{5,1},{9... | collective-permute-start | bytes 1179656 | tf_op jit(solution)/shard_map/while/body/eval_jaxpr/ppermute | solution.py:25
  67.2 12.9 %collective-permute-start = (f32[16,3,16,128]{3,2,1,0:T(8,128)S(1)}, f32[16,3,16,128]{3,2,1,0:T(8,128)S(1)}, u32[]{:S(2)}, u32[]{:S(2)}) collective-permute-start(f32[16,3,16,128]{3,2,1,0:T(8,128)S(1)} %get-tuple-element.321), channel_id=1, source_target_pairs={{4,0},{8,4},{12,8},{16,12},{20,16},{24,20},{28,24},{0,28},{5,1},{9... | collective-permute-start | bytes 1179656 | tf_op jit(solution)/shard_map/while/body/eval_jaxpr/ppermute | solution.py:25
  80.3 12.0 %collective-permute-start = (f32[16,3,16,128]{3,2,1,0:T(8,128)S(1)}, f32[16,3,16,128]{3,2,1,0:T(8,128)S(1)}, u32[]{:S(2)}, u32[]{:S(2)}) collective-permute-start(f32[16,3,16,128]{3,2,1,0:T(8,128)S(1)} %get-tuple-element.321), channel_id=1, source_target_pairs={{4,0},{8,4},{12,8},{16,12},{20,16},{24,20},{28,24},{0,28},{5,1},{9... | collective-permute-start | bytes 1179656 | tf_op jit(solution)/shard_map/while/body/eval_jaxpr/ppermute | solution.py:25
  95.0 10.8 %all-to-all-start = ((f32[4,1,24576]{2,1,0:T(1,128)}), f32[4,1,24576]{2,1,0:T(1,128)S(1)}, u32[]{:S(2)}, u32[]{:S(2)}) async-start(f32[4,1,24576]{2,1,0:T(1,128)} %reshape.519), calls=%async_computation | async-start | bytes 786432 | tf_op jit(solution)/shard_map/all_to_all | solution.py:18
